TPU v7x, 32 devices: a whole 2x2x4 slice. The times are simulated.
32 devices in a mesh: expert: 8 (over z, core), hidden: 4 (over y, x).
Axes of the slice: x: 2, y: 2, z: 4, core: 2. Of those that a mesh axis runs over, the one named last changes fastest.
Arguments:
- inputs: bfloat16 [1536, 2880], P('expert', 'hidden'), may hold values from -6 to 6
- out_grad: bfloat16 [1536, 2880], P('expert', 'hidden'), may hold values from -6 to 6
- expert_ids: int32 [1536, 4], P('expert'), may hold values from 0 to 7, all different within a row; in each aligned block of 192 rows (0 to 191, 192 to 383, ...) at most 144 rows name the same one
- route_weight: float32 [1536, 4], P('expert'), may hold values from 0.1 to 1
- w_gate: bfloat16 [8, 2880, 2880], P('expert', 'hidden'), may hold values from -0.109375 to 0.109375
- w_up: bfloat16 [8, 2880, 2880], P('expert', 'hidden'), may hold values from -0.109375 to 0.109375
- w_down: bfloat16 [8, 2880, 2880], P('expert', 'hidden'), may hold values from -0.109375 to 0.109375
Outputs:
- grad_input: bfloat16 [1536, 2880], P('expert', 'hidden')
- grad_route: float32 [1536, 4], P('expert')
- grad_gate: float32 [8, 2880, 2880], P('expert', 'hidden')
- grad_up: float32 [8, 2880, 2880], P('expert', 'hidden')
- grad_down: float32 [8, 2880, 2880], P('expert', 'hidden')
Inputs may be any that keep to these rules, and one draw needn't show every extreme that they name: `expert_ids`: each token names 4 different experts. Among the 192 tokens of one index of the expert axis no expert is named more than 144 times, a bound that some block reaches.
All inputs are finite; a program needn't handle non-finite values.
Results may differ from a plain program's by a relative error of at most 0.018.
Values may be sent and summed in bfloat16 or wider, within the bound.
No kernel may reach another device: no remote copies, remote signals or barrier semaphores. Data moves between devices by JAX's collectives and lax.ppermute only.
A program may use at most 128 MiB of HBM per device.

v0:
```python
import jax
import jax.numpy as jnp
from jax import lax
from jax.sharding import PartitionSpec as P


def slot_tables(expert_ids, experts, capacity):
    count, top = expert_ids.shape
    flat = expert_ids.reshape(-1)
    onehot = (flat[:, None] == jnp.arange(experts, dtype=jnp.int32)[None, :]).astype(jnp.int32)
    position = jnp.cumsum(onehot, axis=0) - 1
    slot = jnp.sum(onehot * position, axis=1)
    dest = flat * capacity + slot
    table = (
        jnp.zeros((experts * capacity,), jnp.int32)
        .at[dest]
        .set(jnp.arange(count * top, dtype=jnp.int32))
    )
    filled = jnp.zeros((experts * capacity,), jnp.int32).at[dest].set(1)
    return (dest, table, filled)


def pack_rows(values, table, filled, top, experts, capacity):
    picked = values[table // top] * filled.astype(values.dtype)[:, None]
    return picked.reshape(experts, capacity, values.shape[1])


def to_local(buffer, n_groups, local_count):
    rest = buffer.shape[2:]
    shaped = buffer.reshape((n_groups, local_count, buffer.shape[1]) + rest)
    return jnp.swapaxes(shaped, 0, 1).reshape((local_count, n_groups * buffer.shape[1]) + rest)


def from_local(buffer, n_groups, capacity):
    local_count = buffer.shape[0]
    rest = buffer.shape[2:]
    shaped = buffer.reshape((local_count, n_groups, capacity) + rest)
    return jnp.swapaxes(shaped, 0, 1).reshape((n_groups * local_count, capacity) + rest)


def per_device(inputs, out_grad, expert_ids, route_weight, w_gate, w_up, w_down):
    n_groups = lax.axis_size("expert")
    local_count = w_gate.shape[0]
    experts = local_count * n_groups
    tok_count, top = expert_ids.shape
    capacity = 3 * top * tok_count // (2 * experts)
    dest, table, filled = slot_tables(expert_ids, experts, capacity)
    send_weight = (route_weight.reshape(-1)[table] * filled.astype(jnp.float32)).reshape(
        experts, capacity
    )
    send_x = pack_rows(inputs, table, filled, top, experts, capacity)
    send_dy = pack_rows(out_grad, table, filled, top, experts, capacity)
    got_x, got_dy, got_weight = (
        lax.all_to_all(send_x, "expert", split_axis=0, concat_axis=0, tiled=True),
        lax.all_to_all(send_dy, "expert", split_axis=0, concat_axis=0, tiled=True),
        lax.all_to_all(
            send_weight.astype(jnp.bfloat16), "expert", split_axis=0, concat_axis=0, tiled=True
        ).astype(send_weight.dtype),
    )
    rows_x, rows_dy = (
        lax.all_gather(got_x, "hidden", axis=2, tiled=True),
        lax.all_gather(got_dy, "hidden", axis=2, tiled=True),
    )
    xs = to_local(rows_x, n_groups, local_count)
    dys = to_local(rows_dy, n_groups, local_count)
    weights = to_local(got_weight, n_groups, local_count)
    gate = jnp.einsum("esd,efd->esf", xs, w_gate, preferred_element_type=jnp.float32)
    up = jnp.einsum("esd,efd->esf", xs, w_up, preferred_element_type=jnp.float32)
    sig = jax.nn.sigmoid(gate)
    act = gate * sig
    hidden = (act * up).astype(jnp.bfloat16)
    back = jnp.einsum("esd,efd->esf", dys, w_down, preferred_element_type=jnp.float32)
    route_part = jnp.sum(hidden.astype(jnp.float32) * back, axis=2)
    grad_hidden = weights[:, :, None] * back
    scaled = (weights[:, :, None] * dys.astype(jnp.float32)).astype(jnp.bfloat16)
    grad_down = jnp.einsum("esf,esd->efd", hidden, scaled, preferred_element_type=jnp.float32)
    d_gate = (grad_hidden * up * sig * (1.0 + gate * (1.0 - sig))).astype(jnp.bfloat16)
    d_up = (grad_hidden * act).astype(jnp.bfloat16)
    grad_gate = jnp.einsum("esf,esd->efd", d_gate, xs, preferred_element_type=jnp.float32)
    grad_up = jnp.einsum("esf,esd->efd", d_up, xs, preferred_element_type=jnp.float32)
    partial_value = jnp.einsum("esf,efd->esd", d_gate, w_gate, preferred_element_type=jnp.float32)
    partial_value = partial_value + jnp.einsum(
        "esf,efd->esd", d_up, w_up, preferred_element_type=jnp.float32
    )
    route_total = lax.psum(route_part, "hidden")
    route_back = from_local(route_total, n_groups, capacity)
    summed = lax.psum_scatter(
        partial_value.astype(jnp.bfloat16), "hidden", scatter_dimension=2, tiled=True
    ).astype(jnp.float32)
    back_rows, back_route = (
        lax.all_to_all(
            from_local(summed, n_groups, capacity).astype(jnp.bfloat16),
            "expert",
            split_axis=0,
            concat_axis=0,
            tiled=True,
        ).astype(jnp.float32),
        lax.all_to_all(
            route_back.astype(jnp.bfloat16), "expert", split_axis=0, concat_axis=0, tiled=True
        ).astype(route_back.dtype),
    )
    per_pair = back_rows.reshape(experts * capacity, back_rows.shape[2])[dest]
    grad_input = jnp.sum(per_pair.reshape(tok_count, top, per_pair.shape[1]), axis=1).astype(
        jnp.bfloat16
    )
    grad_route = back_route.reshape(-1)[dest].reshape(tok_count, top)
    return (grad_input, grad_route, grad_gate, grad_up, grad_down)


def solution(mesh):
    placed = (
        P("expert", "hidden"),
        P("expert", "hidden"),
        P("expert", None),
        P("expert", None),
        P("expert", "hidden", None),
        P("expert", "hidden", None),
        P("expert", "hidden", None),
    )
    return jax.shard_map(
        per_device,
        mesh=mesh,
        in_specs=placed,
        out_specs=(
            P("expert", "hidden"),
            P("expert", None),
            P("expert", "hidden", None),
            P("expert", "hidden", None),
            P("expert", "hidden", None),
        ),
        check_vma=False,
    )
```

profile of v0, /device:TPU:0, one launch (start us, length us, event | category | flops | bytes accessed | tf_op | source)
XLA Modules:
  0.0 514.7 jit_solution(17609842924973014855)
XLA Ops:
  11.5 3.4 scatter_custom_fusion
  15.0 4.6 gather_fusion.1
  19.5 4.8 gather_fusion.2
  24.4 3.4 scatter_custom_fusion.1
  27.9 3.0 broadcast_multiply_fusion.1
  30.8 48.3 %all_to_all.27 = bf16[8,144,720]{2,1,0:T(8,128)(2,1)} all-to-all(bf16[8,144,720]{2,1,0:T(8,128)(2,1)S(1)} %get-tuple-element.32), channel_id=1, replica_groups=mesh['expert'=8,'hidden'=4] {'expert'}, dimensions={0} | all-to-all | bytes 3317760 | tf_op jit(solution)/shard_map/all_to_all | solution.py:54
  79.1 5.1 copy.57
  84.3 45.2 %all_to_all.28 = bf16[8,144,720]{2,1,0:T(8,128)(2,1)} all-to-all(bf16[8,144,720]{2,1,0:T(8,128)(2,1)S(1)} %copy-done.3), channel_id=1, replica_groups=mesh['expert'=8,'hidden'=4] {'expert'}, dimensions={0} | all-to-all | bytes 3317760 | tf_op jit(solution)/shard_map/all_to_all | solution.py:55
  129.4 5.0 copy.55
  134.8 4.6 gather_fusion
  139.4 8.0 %all_to_all.29 = bf16[8,1,144]{2,1,0:T(2,128)(2,1)S(1)} all-to-all(bf16[8,1,144]{2,1,0:T(2,128)(2,1)S(1)} %convert_element_type.129), channel_id=1, replica_groups=mesh['expert'=8,'hidden'=4] {'expert'}, dimensions={0} | all-to-all | bytes 4608 | tf_op jit(solution)/shard_map/all_to_all | solution.py:56
  147.5 51.6 %all-gather.5.cloned.1.call-done = bf16[8,144,2880]{1,0,2:T(8,128)(2,1)} async-done(((bf16[8,144,720]{1,0,2:T(8,128)(2,1)}), bf16[8,144,2880]{1,0,2:T(8,128)(2,1)}) %all-gather.5.cloned.1.call-update) | async-done | bytes 6635536 | tf_op jit(solution)/shard_map/all_gather | solution.py:61
  199.1 16.3 %copy.58 = bf16[8,144,2880]{2,1,0:T(8,128)(2,1)} copy(bf16[8,144,2880]{1,0,2:T(8,128)(2,1)} %all-gather.5.cloned.1.call-done) | data formatting | bytes 13271040 | tf_op jit(solution)/shard_map/all_gather | solution.py:61
  215.4 11.0 %fusion.10 = f32[1152,720]{0,1:T(8,128)} fusion(bf16[1152,2880]{1,0:T(8,128)(2,1)} %bitcast.60, bf16[1,720,2880]{2,1,0:T(8,128)(2,1)} %param.12), kind=kOutput, calls=%fused_computation.21 | convolution fusion | flops 4777574400 | bytes 14100480 | tf_op jit(solution)/shard_map/esd,efd->esf/dot_general | solution.py:68
  226.4 7.6 %fusion.7 = f32[1152,720]{0,1:T(8,128)} fusion(bf16[1152,2880]{1,0:T(8,128)(2,1)S(1)} %bitcast.63, bf16[1,720,2880]{2,1,0:T(8,128)(2,1)S(1)} %bitcast.69), kind=kOutput, calls=%fused_computation.18 | convolution fusion | flops 4777574400 | bytes 14100480 | tf_op jit(solution)/shard_map/esd,efd->esf/dot_general | solution.py:67
  234.0 82.8 %all-gather.3.cloned.1.call-done = bf16[8,144,2880]{1,0,2:T(8,128)(2,1)} async-done(((bf16[8,144,720]{1,0,2:T(8,128)(2,1)}), bf16[8,144,2880]{1,0,2:T(8,128)(2,1)}) %all-gather.3.cloned.1.call-update) | async-done | bytes 6635536 | tf_op jit(solution)/shard_map/all_gather | solution.py:62
  316.9 15.4 %copy.56 = bf16[8,144,2880]{2,1,0:T(8,128)(2,1)} copy(bf16[8,144,2880]{1,0,2:T(8,128)(2,1)} %all-gather.3.cloned.1.call-done) | data formatting | bytes 13271040 | tf_op jit(solution)/shard_map/all_gather | solution.py:62
  332.2 13.6 %multiply_reduce_fusion = (f32[1152]{0:T(1024)S(1)}, bf16[1152,720]{0,1:T(8,128)(2,1)}, bf16[1152,720]{0,1:T(8,128)(2,1)S(1)}, bf16[1152,720]{0,1:T(8,128)(2,1)}) fusion(f32[1152,720]{0,1:T(8,128)} %fusion.10, f32[1152,720]{0,1:T(8,128)} %fusion.7, f32[1152]{0:T(1024)S(1)} %reshape.232, bf16[1152,2880]{1,0:T(8,128)(2,1)} %bitcast.64, ...), kind=kOutput, calls=%fused_computation.25 | convolution fusion | flops 4793332736 | bytes 22404096 | tf_op jit(solution)/shard_map/esd,efd->esf/dot_general | solution.py:72
  345.9 8.8 %fusion.5 = f32[1152,2880]{0,1:T(8,128)} fusion(bf16[1152,720]{0,1:T(8,128)(2,1)S(1)} %get-tuple-element.27, bf16[1,720,2880]{2,1,0:T(8,128)(2,1)S(1)} %bitcast.71), kind=kOutput, calls=%fused_computation.16 | convolution fusion | flops 4777574400 | bytes 19077120 | tf_op jit(solution)/shard_map/esf,efd->esd/dot_general | solution.py:81
  354.6 15.3 %fusion.1 = bf16[1,1152,2880]{1,2,0:T(8,128)(2,1)} fusion(f32[1152,2880]{0,1:T(8,128)} %fusion.5, bf16[1152,720]{0,1:T(8,128)(2,1)} %get-tuple-element.28, bf16[1,720,2880]{2,1,0:T(8,128)(2,1)} %param.12), kind=kOutput, calls=%fused_computation.10 | convolution fusion | flops 4784209920 | bytes 25712640 | tf_op jit(solution)/shard_map/esf,efd->esd/dot_general | solution.py:82
  370.0 16.9 %psum.7 = bf16[1,1152]{1,0:T(2,128)(2,1)S(1)} all-reduce(f32[1,1152]{1,0:T(1,128)S(1)} %reduce_sum.35), channel_id=1, replica_groups=mesh['expert'=8,'hidden'=4] {'hidden'}, use_global_device_ids=true, to_apply=%region_8.9 | all-reduce | flops 1152 | bytes 6912 | tf_op jit(solution)/shard_map/psum | solution.py:85
  387.6 4.6 all-to-all-start.4
  392.2 11.6 %convolution_bitcast_fusion = f32[1,720,2880]{2,1,0:T(8,128)} fusion(bf16[1152,720]{0,1:T(8,128)(2,1)S(1)} %copy-done.7, bf16[1152,2880]{1,0:T(8,128)(2,1)} %bitcast.61), kind=kOutput, calls=%fused_computation.14 | convolution fusion | flops 4777574400 | bytes 16588800 | tf_op jit(solution)/shard_map/esf,esd->efd/dot_general | solution.py:80
  403.8 40.7 %reduce-scatter.7.cloned.1.call-done = bf16[1,1152,720]{1,2,0:T(8,128)(2,1)} async-done(((bf16[1,1152,2880]{1,2,0:T(8,128)(2,1)}), bf16[1,1152,720]{1,2,0:T(8,128)(2,1)}) %reduce-scatter.7.cloned.1.call-update) | async-done | bytes 1658896
  444.6 3.8 copy.59
  448.4 4.6 all-to-all-start.3
  452.9 11.4 %convolution_bitcast_fusion.1 = f32[1,720,2880]{2,1,0:T(8,128)} fusion(bf16[1152,720]{0,1:T(8,128)(2,1)} %copy-done.6, bf16[1152,2880]{1,0:T(8,128)(2,1)} %bitcast.62), kind=kOutput, calls=%fused_computation.15 | convolution fusion | flops 4777574400 | bytes 16588800 | tf_op jit(solution)/shard_map/esf,esd->efd/dot_general | solution.py:79
  464.3 11.2 %fusion.4 = f32[1,720,2880]{2,1,0:T(8,128)} fusion(bf16[1152,720]{0,1:T(8,128)(2,1)S(1)} %copy-done.8, bf16[1152,2880]{1,0:T(8,128)(2,1)} %bitcast.65, f32[1152]{0:T(1024)S(1)} %reshape.232), kind=kOutput, calls=%fused_computation.13 | convolution fusion | flops 4787527680 | bytes 16593408 | tf_op jit(solution)/shard_map/esf,esd->efd/dot_general | solution.py:76
  475.7 4.5 gather_fusion.4
  480.9 14.0 %all-to-all-done.3 = bf16[8,144,720]{2,1,0:T(8,128)(2,1)S(1)} async-done(((bf16[8,144,720]{2,1,0:T(8,128)(2,1)}), bf16[8,144,720]{2,1,0:T(8,128)(2,1)S(1)}, u32[]{:S(2)}, u32[]{:S(2)}) %all-to-all-start.3) | async-done | bytes 1658912 | tf_op jit(solution)/shard_map/all_to_all | solution.py:91
  497.1 6.1 %gather_fusion.3 = f32[768,720]{1,0:T(8,128)} fusion(f32[1152,720]{1,0:T(8,128)} %bitcast_convert_fusion, s32[1024]{0:T(1024)S(1)} %pad_clamp_fusion.2), kind=kCustom, calls=%fused_computation.3 | custom fusion | bytes 4426752 | tf_op jit(solution)/shard_map/gather | solution.py:102
  503.2 2.6 reshape.230
  (71 shorter events, 11.1 us)
Async XLA Ops:
  7.2 7.8 %copy-start = (bf16[192,720]{1,0:T(8,128)(2,1)S(1)}, bf16[192,720]{1,0:T(8,128)(2,1)}, u32[]{:S(2)}) copy-start(bf16[192,720]{1,0:T(8,128)(2,1)} %param.8) | copy-start | bytes 829444
  7.2 192.0 %all-gather.5.cloned.1.call-start = ((), (), s32[]{:S(2)}) async-start(), calls=%async_computation.7 | async-start | bytes 14745600 | tf_op jit(solution)/shard_map/all_gather | solution.py:61
  15.0 4.6 copy-start.2
  79.1 5.2 %copy-start.3 = (bf16[8,144,720]{2,1,0:T(8,128)(2,1)S(1)}, bf16[8,144,720]{2,1,0:T(8,128)(2,1)}, u32[]{:S(2)}) copy-start(bf16[8,144,720]{2,1,0:T(8,128)(2,1)} %get-tuple-element.31) | copy-start | bytes 4976644
  84.2 232.6 %all-gather.3.cloned.1.call-start = ((), (), s32[]{:S(2)}) async-start(), calls=%async_computation.6 | async-start | bytes 14745600 | tf_op jit(solution)/shard_map/all_gather | solution.py:62
  129.4 5.1 copy-start.5
  134.5 310.1 %reduce-scatter.7.cloned.1.call-start = ((), (), s32[]{:S(2)}) async-start(), calls=%async_computation.8 | async-start | bytes 8294400
  199.1 27.3 %slice-start = ((s8[4239360]{0:T(1024)(128)(4,1)}), s8[45056]{0:T(1024)(128)(4,1)S(1)}, s32[]{:S(2)}) async-start(s8[4239360]{0:T(1024)(128)(4,1)} %bitcast.68), calls=%async_computation.9 | async-start | bytes 90112
  215.4 11.0 %copy-start.4 = (bf16[8,144,2880]{2,1,0:T(8,128)(2,1)S(1)}, bf16[8,144,2880]{2,1,0:T(8,128)(2,1)}, u32[]{:S(2)}) copy-start(bf16[8,144,2880]{2,1,0:T(8,128)(2,1)} %copy.58) | copy-start | bytes 19906564
  215.4 11.0 %slice-start.1 = ((s8[4239360]{0:T(1024)(128)(4,1)}), s8[4194304]{0:T(1024)(128)(4,1)S(1)}, s32[]{:S(2)}) async-start(s8[4239360]{0:T(1024)(128)(4,1)} %bitcast.68), calls=%async_computation.10 | async-start | bytes 8388608
  316.9 29.0 %slice-start.2 = ((s8[4239360]{0:T(1024)(128)(4,1)}), s8[45056]{0:T(1024)(128)(4,1)S(1)}, s32[]{:S(2)}) async-start(s8[4239360]{0:T(1024)(128)(4,1)} %bitcast.70), calls=%async_computation.11 | async-start | bytes 90112
  332.2 13.6 %slice-start.3 = ((s8[4239360]{0:T(1024)(128)(4,1)}), s8[4194304]{0:T(1024)(128)(4,1)S(1)}, s32[]{:S(2)}) async-start(s8[4239360]{0:T(1024)(128)(4,1)} %bitcast.70), calls=%async_computation.12 | async-start | bytes 8388608
  345.8 8.8 %copy-start.6 = (bf16[1152,720]{0,1:T(8,128)(2,1)}, bf16[1152,720]{0,1:T(8,128)(2,1)S(1)}, u32[]{:S(2)}) copy-start(bf16[1152,720]{0,1:T(8,128)(2,1)S(1)} %get-tuple-element.27) | copy-start | bytes 4976644
  370.0 22.3 %copy-start.7 = (bf16[1152,720]{0,1:T(8,128)(2,1)S(1)}, bf16[1152,720]{0,1:T(8,128)(2,1)}, u32[]{:S(2)}) copy-start(bf16[1152,720]{0,1:T(8,128)(2,1)} %get-tuple-element.28) | copy-start | bytes 4976644
  387.6 60.7 %all-to-all-start.4 = ((bf16[8,1,144]{2,1,0:T(2,128)(2,1)}), bf16[8,1,144]{2,1,0:T(2,128)(2,1)S(1)}, u32[]{:S(2)}, u32[]{:S(2)}) async-start(bf16[8,1,144]{2,1,0:T(2,128)(2,1)} %convert_element_type.130), calls=%async_computation.4 | async-start | bytes 16384 | tf_op jit(solution)/shard_map/all_to_all | solution.py:98
  448.4 46.6 %all-to-all-start.3 = ((bf16[8,144,720]{2,1,0:T(8,128)(2,1)}), bf16[8,144,720]{2,1,0:T(8,128)(2,1)S(1)}, u32[]{:S(2)}, u32[]{:S(2)}) async-start(bf16[8,144,720]{2,1,0:T(8,128)(2,1)} %bitcast.11), calls=%async_computation.3 | async-start | bytes 3538944 | tf_op jit(solution)/shard_map/all_to_all | solution.py:91
  452.9 11.4 %copy-start.8 = (bf16[1152,720]{0,1:T(8,128)(2,1)S(1)}, bf16[1152,720]{0,1:T(8,128)(2,1)}, u32[]{:S(2)}) copy-start(bf16[1152,720]{0,1:T(8,128)(2,1)} %get-tuple-element.26) | copy-start | bytes 4976644
  497.1 11.1 %copy-start.1 = (bf16[192,720]{1,0:T(8,128)(2,1)S(1)}, bf16[192,720]{1,0:T(8,128)(2,1)}, u32[]{:S(2)}) copy-start(bf16[192,720]{1,0:T(8,128)(2,1)} %param.8) | copy-start | bytes 829444
Sparse Core Ops, SparseCore 0:
  84.3 114.7 all-gather.4
  201.0 115.8 all-gather.2
  370.1 74.3 reduce-scatter.6
where the time goes:
time: 516 us; the launch traced here: 515 us
  waiting for transfers between devices  189 us (37%)
  blocking collectives  118 us (23%)
  matrix products  90.5 us (18%)
  local copies, waits for them, and re-layouts  83.2 us (16%)
  between operations  14 us (3%)
  other arithmetic  10.2 us (2%)
  starting transfers between devices  9.32 us (2%)
    all_gather x1, waiting for transfers between devices, per_device(): lax.all_gather(got_dy, 'hidden', axis=2, tiled=True)  82.8 us
    all_gather x1, waiting for transfers between devices, per_device(): lax.all_gather(got_x, 'hidden', axis=2, tiled=True)  51.6 us
    all_to_all x1, blocking collectives, per_device(): lax.all_to_all(send_x, 'expert', split_axis=0, concat_axis=0, tiled=True)  48.3 us
    all_to_all x1, blocking collectives, per_device(): lax.all_to_all(send_dy, 'expert', split_axis=0, concat_axis=0, tiled=True)  45.2 us
    unnamed x4, waiting for transfers between devices  40.8 us
    psum x1, blocking collectives, per_device(): route_total = lax.psum(route_part, 'hidden')  16.9 us
    all_gather x1, local copies, waits for them, and re-layouts, per_device(): lax.all_gather(got_x, 'hidden', axis=2, tiled=True)  16.3 us
    all_gather x1, local copies, waits for them, and re-layouts, per_device(): lax.all_gather(got_dy, 'hidden', axis=2, tiled=True)  15.4 us
  transfers between devices with their start and end apart: 5, of which 4 were waited for; matrix products, arithmetic and copies ran while one was open for 17% of the time, Pallas kernels for 0%

commit v1 on v0

--- a/solution.py
+++ b/solution.py
@@ -59,7 +59,15 @@
     )
     rows_x, rows_dy = (
         lax.all_gather(got_x, "hidden", axis=2, tiled=True),
-        lax.all_gather(got_dy, "hidden", axis=2, tiled=True),
+        jnp.concatenate(
+            lax.all_to_all(
+                jnp.stack(lax.psum(1, "hidden") * [got_dy]),
+                axis_name="hidden",
+                split_axis=0,
+                concat_axis=0,
+            ),
+            2,
+        ),
     )
     xs = to_local(rows_x, n_groups, local_count)
     dys = to_local(rows_dy, n_groups, local_count)

time: 516 us -> 512 us (level)
  waiting for transfers between devices: 189 us -> 178 us
  matrix products: 90.5 us -> 80.3 us
  local copies, waits for them, and re-layouts: 83.2 us -> 89.4 us
  starting transfers between devices: 9.32 us -> 15.2 us
    all_to_all x0 -> x1, waiting for transfers between devices: none -> 124 us  [per_device(): lax.all_to_all(jnp.stack(lax.psum(1, 'hidden') * [got_dy]), axis_name='hi...]
    all_gather x1 -> x0, waiting for transfers between devices: 82.8 us -> none  [per_device(): lax.all_gather(got_dy, 'hidden', axis=2, tiled=True)]
    all_gather x1, waiting for transfers between devices: 51.6 us -> 0.01 us  [per_device(): lax.all_gather(got_x, 'hidden', axis=2, tiled=True)]
    another operation x1 -> x3, local copies, waits for them, and re-layouts: 0.08 us -> 17.5 us
    all_gather x1 -> x0, local copies, waits for them, and re-layouts: 15.4 us -> none  [per_device(): lax.all_gather(got_dy, 'hidden', axis=2, tiled=True)]
    reshape x0 -> x1, local copies, waits for them, and re-layouts: none -> 11.4 us  [per_device(): jnp.concatenate(lax.all_to_all(jnp.stack(lax.psum(1, 'hidden') * [got_dy]...]
    all_to_all x0 -> x1, starting transfers between devices: none -> 5.48 us  [per_device(): lax.all_to_all(jnp.stack(lax.psum(1, 'hidden') * [got_dy]), axis_name='hi...]
    dot_general x1, matrix products: 13.6 us -> 8.4 us  [per_device(): jnp.einsum('esd,efd->esf', dys, w_down, preferred_element_type=jnp.float32)]
  transfers between devices with their start and end apart: 5 -> 5, of which waited for: 4 -> 3; matrix products, arithmetic and copies ran while one was open for 17% -> 15% of each run, Pallas kernels for 0% -> 0%
where the time goes in v1:
time: 512 us; the launch traced here: 506 us
  waiting for transfers between devices  178 us (35%)
  blocking collectives  117 us (23%)
  local copies, waits for them, and re-layouts  89.4 us (17%)
  matrix products  80.3 us (16%)
  starting transfers between devices  15.2 us (3%)
  between operations  14.7 us (3%)
  other arithmetic  10.2 us (2%)
    all_to_all x1, waiting for transfers between devices, per_device(): lax.all_to_all(jnp.stack(lax.psum(1, 'hidden') * [got_dy]), axis_name='hi...  124 us
    all_to_all x1, blocking collectives, per_device(): lax.all_to_all(send_x, 'expert', split_axis=0, concat_axis=0, tiled=True)  48.1 us
    all_to_all x1, blocking collectives, per_device(): lax.all_to_all(send_dy, 'expert', split_axis=0, concat_axis=0, tiled=True)  44.4 us
    unnamed x3, waiting for transfers between devices  40.7 us
    psum x1, blocking collectives, per_device(): route_total = lax.psum(route_part, 'hidden')  16.9 us
    all_gather x1, local copies, waits for them, and re-layouts, per_device(): lax.all_gather(got_x, 'hidden', axis=2, tiled=True)  15.8 us
    all_to_all x1, waiting for transfers between devices, per_device(): lax.all_to_all(from_local(summed, n_groups, capacity).astype(jnp.bfloat16...  14 us
    another operation x2, local copies, waits for them, and re-layouts  14 us
  transfers between devices with their start and end apart: 5, of which 3 were waited for; matrix products, arithmetic and copies ran while one was open for 15% of the time, Pallas kernels for 0%

profile of v1, /device:TPU:0, one launch (start us, length us, event | category | flops | bytes accessed | tf_op | source)
XLA Modules:
  0.0 505.7 jit_solution(8519041865845613711)
XLA Ops:
  11.5 3.4 scatter_custom_fusion
  15.0 3.4 scatter_custom_fusion.1
  18.5 4.6 gather_fusion.1
  23.1 4.8 gather_fusion.2
  27.9 3.0 broadcast_multiply_fusion.1
  30.9 48.1 %all_to_all.32 = bf16[8,144,720]{2,1,0:T(8,128)(2,1)S(1)} all-to-all(bf16[8,144,720]{2,1,0:T(8,128)(2,1)S(1)} %get-tuple-element.32), channel_id=1, replica_groups=mesh['expert'=8,'hidden'=4] {'expert'}, dimensions={0} | all-to-all | bytes 3317760 | tf_op jit(solution)/shard_map/all_to_all | solution.py:54
  79.0 3.4 copy.59
  82.7 4.6 gather_fusion
  87.4 8.0 %all_to_all.33 = bf16[8,1,144]{2,1,0:T(2,128)(2,1)S(1)} all-to-all(bf16[8,1,144]{2,1,0:T(2,128)(2,1)S(1)} %convert_element_type.129), channel_id=1, replica_groups=mesh['expert'=8,'hidden'=4] {'expert'}, dimensions={0} | all-to-all | bytes 4608 | tf_op jit(solution)/shard_map/all_to_all | solution.py:56
  95.4 44.4 %all_to_all.34 = bf16[8,144,720]{2,1,0:T(8,128)(2,1)S(1)} all-to-all(bf16[8,144,720]{2,1,0:T(8,128)(2,1)S(1)} %copy-done.3), channel_id=1, replica_groups=mesh['expert'=8,'hidden'=4] {'expert'}, dimensions={0} | all-to-all | bytes 3317760 | tf_op jit(solution)/shard_map/all_to_all | solution.py:55
  139.8 3.5 stack.2
  143.3 5.5 %all-to-all-start.2 = ((bf16[4,8,144,720]{3,2,1,0:T(8,128)(2,1)}), bf16[4,8,144,720]{3,2,1,0:T(8,128)(2,1)}, u32[]{:S(2)}, u32[]{:S(2)}) async-start(bf16[4,8,144,720]{3,2,1,0:T(8,128)(2,1)} %stack.2), calls=%async_computation.2 | async-start | bytes 14155776 | tf_op jit(solution)/shard_map/all_to_all | solution.py:63
  149.4 123.6 %all-to-all-done.2 = bf16[4,8,144,720]{3,2,1,0:T(8,128)(2,1)} async-done(((bf16[4,8,144,720]{3,2,1,0:T(8,128)(2,1)}), bf16[4,8,144,720]{3,2,1,0:T(8,128)(2,1)}, u32[]{:S(2)}, u32[]{:S(2)}) %all-to-all-start.2) | async-done | bytes 6635552 | tf_op jit(solution)/shard_map/all_to_all | solution.py:63
  273.0 11.4 %copy.58 = bf16[8,144,4,720]{3,2,1,0:T(4,128)(2,1)} copy(bf16[8,144,4,720]{3,1,0,2:T(8,128)(2,1)} %bitcast.4) | data formatting | bytes 13271040 | tf_op jit(solution)/shard_map/reshape | solution.py:62
  284.5 13.9 %reshape.229 = bf16[1152,2880]{1,0:T(8,128)(2,1)} reshape(bf16[8,144,4,720]{3,2,1,0:T(4,128)(2,1)} %copy.58) | data formatting | bytes 13271040 | tf_op jit(solution)/shard_map/reshape.5
  298.3 15.8 %copy.60 = bf16[8,144,2880]{2,1,0:T(8,128)(2,1)} copy(bf16[8,144,2880]{1,0,2:T(8,128)(2,1)} %all-gather.2.cloned.1.call-done) | data formatting | bytes 13271040 | tf_op jit(solution)/shard_map/all_gather | solution.py:61
  314.1 9.8 %fusion.10 = f32[1152,720]{0,1:T(8,128)S(1)} fusion(bf16[1152,2880]{1,0:T(8,128)(2,1)} %bitcast.60, bf16[1,720,2880]{2,1,0:T(8,128)(2,1)} %param.12), kind=kOutput, calls=%fused_computation.21 | convolution fusion | flops 4777574400 | bytes 14100480 | tf_op jit(solution)/shard_map/esd,efd->esf/dot_general | solution.py:76
  324.0 5.9 %fusion.7 = f32[1152,720]{0,1:T(8,128)S(1)} fusion(bf16[1152,2880]{1,0:T(8,128)(2,1)S(1)} %bitcast.63, bf16[1,720,2880]{2,1,0:T(8,128)(2,1)S(1)} %bitcast.71), kind=kOutput, calls=%fused_computation.18 | convolution fusion | flops 4777574400 | bytes 14100480 | tf_op jit(solution)/shard_map/esd,efd->esf/dot_general | solution.py:75
  330.0 8.4 %multiply_reduce_fusion = (f32[1152]{0:T(1024)S(1)}, bf16[1152,720]{0,1:T(8,128)(2,1)}, bf16[1152,720]{0,1:T(8,128)(2,1)S(1)}, bf16[1152,720]{0,1:T(8,128)(2,1)S(1)}) fusion(f32[1152,720]{0,1:T(8,128)S(1)} %fusion.10, f32[1152,720]{0,1:T(8,128)S(1)} %fusion.7, f32[1152]{0:T(1024)S(1)} %reshape.238, bf16[1152,2880]{1,0:T(8,128)(2,1)S(1)} %bitcast.65, ...), kind=kOutput, calls=%fused_computation.25 | convolution fusion | flops 4793332736 | bytes 22404096 | tf_op jit(solution)/shard_map/esd,efd->esf/dot_general | solution.py:80
  338.4 8.7 %fusion.5 = f32[1152,2880]{0,1:T(8,128)} fusion(bf16[1152,720]{0,1:T(8,128)(2,1)S(1)} %get-tuple-element.27, bf16[1,720,2880]{2,1,0:T(8,128)(2,1)S(1)} %bitcast.71), kind=kOutput, calls=%fused_computation.16 | convolution fusion | flops 4777574400 | bytes 19077120 | tf_op jit(solution)/shard_map/esf,efd->esd/dot_general | solution.py:89
  347.1 13.3 %fusion.1 = bf16[1,1152,2880]{1,2,0:T(8,128)(2,1)} fusion(f32[1152,2880]{0,1:T(8,128)} %fusion.5, bf16[1152,720]{0,1:T(8,128)(2,1)S(1)} %get-tuple-element.28, bf16[1,720,2880]{2,1,0:T(8,128)(2,1)} %param.12), kind=kOutput, calls=%fused_computation.10 | convolution fusion | flops 4784209920 | bytes 25712640 | tf_op jit(solution)/shard_map/esf,efd->esd/dot_general | solution.py:90
  360.4 16.9 %psum.7 = bf16[1,1152]{1,0:T(2,128)(2,1)S(1)} all-reduce(f32[1,1152]{1,0:T(1,128)S(1)} %reduce_sum.35), channel_id=1, replica_groups=mesh['expert'=8,'hidden'=4] {'hidden'}, use_global_device_ids=true, to_apply=%region_8.9 | all-reduce | flops 1152 | bytes 6912 | tf_op jit(solution)/shard_map/psum | solution.py:93
  378.1 4.6 all-to-all-start.5
  382.6 11.6 %convolution_bitcast_fusion.1 = f32[1,720,2880]{2,1,0:T(8,128)} fusion(bf16[1152,720]{0,1:T(8,128)(2,1)S(1)} %copy-done.8, bf16[1152,2880]{1,0:T(8,128)(2,1)} %bitcast.61), kind=kOutput, calls=%fused_computation.15 | convolution fusion | flops 4777574400 | bytes 16588800 | tf_op jit(solution)/shard_map/esf,esd->efd/dot_general | solution.py:87
  394.2 40.7 %reduce-scatter.7.cloned.1.call-done = bf16[1,1152,720]{1,2,0:T(8,128)(2,1)} async-done(((bf16[1,1152,2880]{1,2,0:T(8,128)(2,1)}), bf16[1,1152,720]{1,2,0:T(8,128)(2,1)}) %reduce-scatter.7.cloned.1.call-update) | async-done | bytes 1658896
  435.0 3.8 copy.61
  438.8 4.6 all-to-all-start.4
  443.4 11.4 %convolution_bitcast_fusion = f32[1,720,2880]{2,1,0:T(8,128)} fusion(bf16[1152,720]{0,1:T(8,128)(2,1)} %copy-done.6, bf16[1152,2880]{1,0:T(8,128)(2,1)} %bitcast.62), kind=kOutput, calls=%fused_computation.14 | convolution fusion | flops 4777574400 | bytes 16588800 | tf_op jit(solution)/shard_map/esf,esd->efd/dot_general | solution.py:88
  454.8 11.2 %fusion.4 = f32[1,720,2880]{2,1,0:T(8,128)} fusion(bf16[1152,720]{0,1:T(8,128)(2,1)S(1)} %copy-done.9, bf16[1152,2880]{1,0:T(8,128)(2,1)} %reshape.229, f32[1152]{0:T(1024)S(1)} %reshape.238), kind=kOutput, calls=%fused_computation.13 | convolution fusion | flops 4787527680 | bytes 16593408 | tf_op jit(solution)/shard_map/esf,esd->efd/dot_general | solution.py:84
  466.1 4.5 gather_fusion.4
  471.4 14.0 %all-to-all-done.4 = bf16[8,144,720]{2,1,0:T(8,128)(2,1)S(1)} async-done(((bf16[8,144,720]{2,1,0:T(8,128)(2,1)}), bf16[8,144,720]{2,1,0:T(8,128)(2,1)S(1)}, u32[]{:S(2)}, u32[]{:S(2)}) %all-to-all-start.4) | async-done | bytes 1658912 | tf_op jit(solution)/shard_map/all_to_all | solution.py:99
  487.5 6.1 %gather_fusion.3 = f32[768,720]{1,0:T(8,128)} fusion(f32[1152,720]{1,0:T(8,128)} %bitcast_convert_fusion, s32[1024]{0:T(1024)S(1)} %pad_clamp_fusion.2), kind=kCustom, calls=%fused_computation.3 | custom fusion | bytes 4426752 | tf_op jit(solution)/shard_map/gather | solution.py:110
  (78 shorter events, 14.1 us)
Async XLA Ops:
  7.2 11.3 %copy-start = (bf16[192,720]{1,0:T(8,128)(2,1)S(1)}, bf16[192,720]{1,0:T(8,128)(2,1)}, u32[]{:S(2)}) copy-start(bf16[192,720]{1,0:T(8,128)(2,1)} %param.8) | copy-start | bytes 829444
  7.2 291.2 %all-gather.2.cloned.1.call-start = ((), (), s32[]{:S(2)}) async-start(), calls=%async_computation.7 | async-start | bytes 14745600 | tf_op jit(solution)/shard_map/all_gather | solution.py:61
  18.5 4.6 copy-start.2
  79.0 3.4 copy-start.5
  82.7 12.7 %copy-start.3 = (bf16[8,144,720]{2,1,0:T(8,128)(2,1)S(1)}, bf16[8,144,720]{2,1,0:T(8,128)(2,1)}, u32[]{:S(2)}) copy-start(bf16[8,144,720]{2,1,0:T(8,128)(2,1)} %get-tuple-element.31) | copy-start | bytes 4976644
  143.3 129.7 %all-to-all-start.2 = ((bf16[4,8,144,720]{3,2,1,0:T(8,128)(2,1)}), bf16[4,8,144,720]{3,2,1,0:T(8,128)(2,1)}, u32[]{:S(2)}, u32[]{:S(2)}) async-start(bf16[4,8,144,720]{3,2,1,0:T(8,128)(2,1)} %stack.2), calls=%async_computation.2 | async-start | bytes 14155776 | tf_op jit(solution)/shard_map/all_to_all | solution.py:63
  148.8 286.2 %reduce-scatter.7.cloned.1.call-start = ((), (), s32[]{:S(2)}) async-start(), calls=%async_computation.8 | async-start | bytes 8294400
  298.3 25.6 %slice-start.4 = ((s8[4239360]{0:T(1024)(128)(4,1)}), s8[45056]{0:T(1024)(128)(4,1)S(1)}, s32[]{:S(2)}) async-start(s8[4239360]{0:T(1024)(128)(4,1)} %bitcast.70), calls=%async_computation.13 | async-start | bytes 90112
  314.1 9.9 %copy-start.4 = (bf16[8,144,2880]{2,1,0:T(8,128)(2,1)S(1)}, bf16[8,144,2880]{2,1,0:T(8,128)(2,1)}, u32[]{:S(2)}) copy-start(bf16[8,144,2880]{2,1,0:T(8,128)(2,1)} %copy.60) | copy-start | bytes 19906564
  314.1 9.9 %slice-start.5 = ((s8[4239360]{0:T(1024)(128)(4,1)}), s8[4194304]{0:T(1024)(128)(4,1)S(1)}, s32[]{:S(2)}) async-start(s8[4239360]{0:T(1024)(128)(4,1)} %bitcast.70), calls=%async_computation.14 | async-start | bytes 8388608
  314.1 15.8 %slice-start = ((s8[6782976]{0:T(1024)(128)(4,1)}), s8[4194304]{0:T(1024)(128)(4,1)S(1)}, s32[]{:S(2)}) async-start(s8[6782976]{0:T(1024)(128)(4,1)} %bitcast.64), calls=%async_computation.9 | async-start | bytes 8388608
  314.1 15.8 %slice-start.2 = ((s8[4239360]{0:T(1024)(128)(4,1)}), s8[4194304]{0:T(1024)(128)(4,1)S(1)}, s32[]{:S(2)}) async-start(s8[4239360]{0:T(1024)(128)(4,1)} %bitcast.68), calls=%async_computation.11 | async-start | bytes 8388608
  324.0 5.9 %slice-start.1 = ((s8[6782976]{0:T(1024)(128)(4,1)}), s8[2588672]{0:T(1024)(128)(4,1)S(1)}, s32[]{:S(2)}) async-start(s8[6782976]{0:T(1024)(128)(4,1)} %bitcast.64), calls=%async_computation.10 | async-start | bytes 5177344
  324.0 5.9 %slice-start.3 = ((s8[4239360]{0:T(1024)(128)(4,1)}), s8[45056]{0:T(1024)(128)(4,1)S(1)}, s32[]{:S(2)}) async-start(s8[4239360]{0:T(1024)(128)(4,1)} %bitcast.68), calls=%async_computation.12 | async-start | bytes 90112
  338.4 8.7 %copy-start.7 = (bf16[1152,720]{0,1:T(8,128)(2,1)}, bf16[1152,720]{0,1:T(8,128)(2,1)S(1)}, u32[]{:S(2)}) copy-start(bf16[1152,720]{0,1:T(8,128)(2,1)S(1)} %get-tuple-element.27) | copy-start | bytes 4976644
  338.4 8.7 %copy-start.6 = (bf16[1152,720]{0,1:T(8,128)(2,1)}, bf16[1152,720]{0,1:T(8,128)(2,1)S(1)}, u32[]{:S(2)}) copy-start(bf16[1152,720]{0,1:T(8,128)(2,1)S(1)} %get-tuple-element.28) | copy-start | bytes 4976644
  360.4 22.3 %copy-start.8 = (bf16[1152,720]{0,1:T(8,128)(2,1)S(1)}, bf16[1152,720]{0,1:T(8,128)(2,1)}, u32[]{:S(2)}) copy-start(bf16[1152,720]{0,1:T(8,128)(2,1)} %copy-done.7) | copy-start | bytes 4976644
  378.1 60.7 %all-to-all-start.5 = ((bf16[8,1,144]{2,1,0:T(2,128)(2,1)}), bf16[8,1,144]{2,1,0:T(2,128)(2,1)S(1)}, u32[]{:S(2)}, u32[]{:S(2)}) async-start(bf16[8,1,144]{2,1,0:T(2,128)(2,1)} %convert_element_type.130), calls=%async_computation.5 | async-start | bytes 16384 | tf_op jit(solution)/shard_map/all_to_all | solution.py:106
  438.8 46.6 %all-to-all-start.4 = ((bf16[8,144,720]{2,1,0:T(8,128)(2,1)}), bf16[8,144,720]{2,1,0:T(8,128)(2,1)S(1)}, u32[]{:S(2)}, u32[]{:S(2)}) async-start(bf16[8,144,720]{2,1,0:T(8,128)(2,1)} %bitcast.11), calls=%async_computation.4 | async-start | bytes 3538944 | tf_op jit(solution)/shard_map/all_to_all | solution.py:99
  443.4 11.4 %copy-start.9 = (bf16[1152,720]{0,1:T(8,128)(2,1)S(1)}, bf16[1152,720]{0,1:T(8,128)(2,1)}, u32[]{:S(2)}) copy-start(bf16[1152,720]{0,1:T(8,128)(2,1)} %get-tuple-element.26) | copy-start | bytes 4976644
  487.5 11.1 %copy-start.1 = (bf16[192,720]{1,0:T(8,128)(2,1)S(1)}, bf16[192,720]{1,0:T(8,128)(2,1)}, u32[]{:S(2)}) copy-start(bf16[192,720]{1,0:T(8,128)(2,1)} %param.8) | copy-start | bytes 829444
Sparse Core Ops, SparseCore 0:
  82.6 190.6 all-gather.1
  360.5 74.3 reduce-scatter.6
